TPU v7x, 256 devices: a whole 4x4x8 slice. The times are simulated.
256 devices in a mesh: shot: 32 (over z, y_hi, core), ap: 8 (over x, y_lo).
Axes of the slice: x: 4, y: 4 (y_hi: 2, y_lo: 2; y = y_hi * 2 + y_lo), z: 8, core: 2. Of those that a mesh axis runs over, the one named last changes fastest.
Arguments:
- velocity_tiles: float32 [512, 64, 1024], P('shot', 'ap'), may hold values from 1.5 to 4.5
- aperture_tiles: int32 [32, 16], replicated, may hold values from 0 to 511, as said below
- source_cells: int32 [32], P('shot'), may hold values from 0 to 1048575
- wavelet: float32 [32, 6], P('shot'), may hold values from -48 to 48
- receiver_cells: int32 [32, 256], P('shot'), may hold values from 0 to 1048575
- observed: float32 [32, 6, 256], P('shot'), may hold values from -24 to 24
- field_early: float32 [32, 64, 128, 128], P('shot', 'ap'), may hold values from -6 to 6
- field_late: float32 [32, 64, 128, 128], P('shot', 'ap'), may hold values from -6 to 6
- adjoint_late: float32 [32, 64, 128, 128], P('shot', 'ap'), may hold values from -6 to 6
- adjoint_later: float32 [32, 64, 128, 128], P('shot', 'ap'), may hold values from -6 to 6
Outputs:
- grad_tiles: float32 [512, 64, 1024], P('shot', 'ap')
Inputs may be any that keep to these rules, and one draw needn't show every extreme that they name: `aperture_tiles`: the 16 tiles of one shot belong to 16 different owners, tile t being owned by index t // 16 of shot; some owners appear in far more shots than others.
All inputs are finite; a program needn't handle non-finite values.
Results may differ from a plain program's by a relative error of at most 0.0003.
Values sent between devices are 32-bit elements; how exact they have to be, the bound alone decides.
A program may use at most 64 MiB of HBM per device.

v0:
```python
import functools

import jax
import jax.numpy as jnp
from jax import lax
from jax.experimental import pallas as pl
from jax.experimental.pallas import tpu as pltpu
from jax.sharding import PartitionSpec as P

COEF = (-205.0 / 72.0, 8.0 / 5.0, -1.0 / 5.0, 8.0 / 315.0, -1.0 / 560.0)
STEP_SQUARE = 0.01
MESH = pl.DeviceIdType.MESH
STEPS = 6
F32 = jnp.float32
BF16 = jnp.bfloat16
Z_ORDER = (4, 3, 5, 2, 6, 1, 7, 0)


def ap_of(half, quarter):
    mirror = quarter // 2
    y = ((quarter + 1) // 2) % 2
    x = mirror + half * (1 - 2 * mirror)
    return 4 * half + 2 * x + y


def split(value):
    high = value.astype(BF16)
    return high, (value - high.astype(F32)).astype(BF16)


def kernel(
    meta, wav, cells, observed, vel, early, late, a_late, a_later, out,
    fwd, adj, upd, inj, coef, count, image, lap, turn, ymat, hot,
    xs, xr, vsend, vrecv, vpiece, vtile, gtile, gpiece, gsend, grecv,
    f_send, f_recv, f_loc, z_send, z_recv, x_send, x_recv,
    v_send, v_recv, g_send, g_recv, t_send, t_recv, p_send, p_recv,
):
    shots = lax.axis_size("shot")
    me = lax.axis_index("shot")
    ap = lax.axis_index("ap")
    half = ap // 4
    slab = ap % 4
    xl = slab // 2
    yl = slab % 2
    mirror = xl + half * (1 - 2 * xl)
    quarter = yl + mirror * (3 - 2 * yl)
    has_low = quarter > 0
    has_high = quarter < 3

    @pl.loop(1, 7)
    def _(n):
        for buf in (fwd, adj):
            buf[n, 0:4, 8:40, :] = jnp.zeros((4, 32, 128), F32)
            buf[n, 36:40, 8:40, :] = jnp.zeros((4, 32, 128), F32)

    fields = ((late, fwd, 1), (early, fwd, 0), (a_late, adj, 6), (a_later, adj, 7))

    def own_copy(f):
        source, buf, n = fields[f]
        return pltpu.make_async_copy(
            source.at[0, :, pl.ds(32 * quarter, 32), :],
            buf.at[n, pl.ds(4 + 8 * slab, 8), pl.ds(8, 32), :],
            f_loc.at[f],
        )

    def field_copy(f, i):
        source, buf, n = fields[f]
        other = (quarter + i) % 4
        return pltpu.make_async_remote_copy(
            src_ref=source.at[0, :, pl.ds(32 * other, 32), :],
            dst_ref=buf.at[n, pl.ds(4 + 8 * slab, 8), pl.ds(8, 32), :],
            send_sem=f_send.at[f, i - 1],
            recv_sem=f_recv.at[f, i - 1],
            device_id={"ap": ap_of(half, other)},
            device_id_type=MESH,
        )

    for f in range(4):
        own_copy(f).start()

    barrier = pltpu.get_barrier_semaphore()

    @pl.loop(1, shots)
    def _(d):
        pl.semaphore_signal(
            barrier, inc=1, device_id={"shot": (me + d) % shots}, device_id_type=MESH
        )

    for i in range(1, 4):
        pl.semaphore_signal(
            barrier, inc=1, device_id={"ap": ap_of(half, (quarter + i) % 4)}, device_id_type=MESH
        )
    partner = ap_of(1 - half, quarter)
    pl.semaphore_signal(barrier, inc=1, device_id={"ap": partner}, device_id_type=MESH)

    @pl.loop(0, shots)
    def _(s):
        vsend[s] = vel[meta[s]]

    vrecv[me] = vel[meta[me]]

    pl.semaphore_wait(barrier, shots - 1 + 4)

    for f in (0, 1):
        for i in range(1, 4):
            field_copy(f, i).start()

    def exchange_copy(src, dst, target, send, recv):
        return pltpu.make_async_remote_copy(
            src_ref=src.at[target],
            dst_ref=dst.at[me],
            send_sem=send.at[target],
            recv_sem=recv.at[me],
            device_id={"shot": target},
            device_id_type=MESH,
        )

    def arrival(src, dst, origin, send, recv):
        return pltpu.make_async_remote_copy(
            src_ref=src.at[origin],
            dst_ref=dst.at[origin],
            send_sem=send.at[origin],
            recv_sem=recv.at[origin],
            device_id={"shot": origin},
            device_id_type=MESH,
        )

    def exchange_start(src, dst, send, recv):
        planes = shots // 4
        for core in range(2):
            for dz in range(planes):
                for dy in range(2):
                    step = Z_ORDER[dz] if planes == 8 else dz
                    target = (
                        ((me // 4 + step) % planes) * 4 + ((me // 2 + dy) % 2) * 2 + core
                    )

                    @pl.when(target != me)
                    def _():
                        exchange_copy(src, dst, target, send, recv).start()

    exchange_start(vsend, vrecv, v_send, v_recv)

    for f in (2, 3):
        for i in range(1, 4):
            field_copy(f, i).start()

    distance = jnp.abs(
        lax.broadcasted_iota(jnp.int32, (128, 128), 0)
        - lax.broadcasted_iota(jnp.int32, (128, 128), 1)
    )
    band = jnp.where(distance == 0, 3.0 * COEF[0], 0.0)
    for k in range(1, 5):
        band = jnp.where(distance == k, COEF[k], band)
    band_high, band_low = split(band)
    ymat[0:128, 0:128] = band_high
    ymat[128:256, 0:128] = band_high
    ymat[0:128, 128:256] = band_low
    ymat[128:256, 128:256] = jnp.zeros((128, 128), BF16)

    @pl.loop(1, 7)
    def _(n):
        @pl.loop(0, 8)
        def _(g):
            for buf in (fwd, adj):
                buf[n, pl.ds(4 + 4 * g, 4), 0:8, :] = jnp.zeros((4, 8, 128), F32)
                buf[n, pl.ds(4 + 4 * g, 4), 40:48, :] = jnp.zeros((4, 8, 128), F32)

    flat = cells[0:1, :]
    z_at = flat // 16384 - 32 * half
    x_at = (flat // 128) % 128 - 32 * quarter
    y_at = flat % 128
    inside = (z_at >= 0) & (z_at < 32) & (x_at >= 0) & (x_at < 32)
    row_at = jnp.where(inside, z_at * 32 + x_at, -1)
    nrec = cells.shape[1]

    @pl.loop(0, 16)
    def _(b):
        rows = lax.broadcasted_iota(jnp.int32, (64, nrec), 0) + b * 64
        hot[pl.ds(b * 64, 64), :] = jnp.where(rows == row_at, 1.0, 0.0).astype(BF16)

    lanes = jnp.where(
        lax.broadcasted_iota(jnp.int32, (128, nrec), 0) == y_at, 1.0, 0.0
    )
    contract = (((1,), (1,)), ((), ()))
    lanes_low = lanes.astype(BF16)

    @pl.loop(0, 4)
    def _(b):
        found = lax.dot_general(
            hot[pl.ds(b * 256, 256), :], lanes_low, contract, preferred_element_type=F32
        )
        count[pl.ds(8 * b, 8), :, :] = found.reshape(8, 32, 128)

    for n in range(STEPS):
        high, low = split(lanes * observed[0, n : n + 1, :])
        both = jnp.concatenate([high, low], axis=0)

        @pl.loop(0, 4)
        def _(b):
            found = lax.dot_general(
                hot[pl.ds(b * 256, 256), :], both, contract, preferred_element_type=F32
            )
            inj[n, pl.ds(8 * b, 8), :, :] = (found[:, 0:128] + found[:, 128:256]).reshape(
                8, 32, 128
            )

    def z_copy(buf, n, e):
        return pltpu.make_async_remote_copy(
            src_ref=buf.at[n, pl.ds(32 - 28 * half, 4), pl.ds(8, 32), :],
            dst_ref=buf.at[n, pl.ds(36 * half, 4), pl.ds(8, 32), :],
            send_sem=z_send.at[e],
            recv_sem=z_recv.at[e],
            device_id={"ap": partner},
            device_id_type=MESH,
        )

    def x_copy(e, side, c):
        other = ap_of(half, quarter + (2 * side - 1))
        return pltpu.make_async_remote_copy(
            src_ref=xs.at[e, side, pl.ds(8 * c, 8)],
            dst_ref=xr.at[e, 1 - side, pl.ds(8 * c, 8)],
            send_sem=x_send.at[e, side, c],
            recv_sem=x_recv.at[e, 1 - side, c],
            device_id={"ap": other},
            device_id_type=MESH,
        )

    def x_arrival(e, side, c):
        other = ap_of(half, quarter + (2 * side - 1))
        return pltpu.make_async_remote_copy(
            src_ref=xs.at[e, side, pl.ds(8 * c, 8)],
            dst_ref=xr.at[e, side, pl.ds(8 * c, 8)],
            send_sem=x_send.at[e, side, c],
            recv_sem=x_recv.at[e, side, c],
            device_id={"ap": other},
            device_id_type=MESH,
        )

    def x_post(buf, n, e, c):
        at = pl.ds(4 + 8 * c, 8)

        @pl.when(has_low)
        def _():
            xs[e, 0, pl.ds(8 * c, 8)] = buf[n, at, 8:12, :]
            x_copy(e, 0, c).start()

        @pl.when(has_high)
        def _():
            xs[e, 1, pl.ds(8 * c, 8)] = buf[n, at, 36:40, :]
            x_copy(e, 1, c).start()

    def x_take(buf, n, e, c):
        at = pl.ds(4 + 8 * c, 8)

        @pl.when(has_low)
        def _():
            x_arrival(e, 0, c).wait_recv()
            buf[n, at, 4:8, :] = xr[e, 0, pl.ds(8 * c, 8)]

        @pl.when(has_high)
        def _():
            x_arrival(e, 1, c).wait_recv()
            buf[n, at, 40:44, :] = xr[e, 1, pl.ds(8 * c, 8)]

    def chunk_at(i):
        return i * half + (3 - i) * (1 - half)

    def fields_ready(f):
        own_copy(f).wait()
        for i in range(1, 4):
            field_copy(f, i).wait_recv()

    def lateral(buf, n):
        @pl.loop(0, 4)
        def _(c):
            here = buf[n, pl.ds(4 + 8 * c, 8), 8:40, :].reshape(256, 128)
            both = jnp.concatenate(split(here), axis=1)
            found = jnp.dot(both, ymat[...], preferred_element_type=F32)
            lap[pl.ds(8 * c, 8), :, :] = (found[:, 0:128] + found[:, 128:256]).reshape(8, 32, 128)

    for f, e in ((0, 0), (2, 6)):
        buf, n = fields[f][1:]
        fields_ready(f)
        z_copy(buf, n, e).start()
        for i in range(4):
            x_post(buf, n, e, chunk_at(i))
    fields_ready(1)
    fields_ready(3)
    lateral(fwd, 1)

    @pl.loop(0, shots)
    def _(s):
        @pl.when(s != me)
        def _():
            arrival(vsend, vrecv, s, v_send, v_recv).wait_recv()

    @pl.loop(0, 16)
    def _(k):
        vpiece[k] = vrecv[meta[2 * shots + k]]

    def tile_copy(i):
        other = (quarter + i) % 4
        return pltpu.make_async_remote_copy(
            src_ref=vpiece.at[pl.ds(4 * other, 4)],
            dst_ref=vtile.at[slab],
            send_sem=t_send.at[i - 1],
            recv_sem=t_recv.at[i - 1],
            device_id={"ap": ap_of(half, other)},
            device_id_type=MESH,
        )

    for i in range(1, 4):
        tile_copy(i).start()
    vtile[slab] = vpiece[pl.ds(4 * quarter, 4)]
    for i in range(1, 4):
        tile_copy(i).wait_recv()

    lane_block = lax.broadcasted_iota(jnp.int32, (8, 128), 1) // 32

    @pl.loop(0, 4)
    def _(j):
        for a in range(8):
            tiles = [vtile[j, ky, :, 128 * a : 128 * a + 128] for ky in range(4)]
            for b in range(4):
                joined = None
                for ky in range(4):
                    shift = (32 * (ky - b)) % 128
                    moved = pltpu.roll(tiles[ky], shift, 1) if shift else tiles[ky]
                    joined = moved if joined is None else jnp.where(lane_block == ky, moved, joined)
                turn[8 * (4 * a + b) : 8 * (4 * a + b) + 8, :] = joined
        for z in range(8):
            for x in range(0, 32, 8):
                speed = turn[pl.ds(8 * x + z, 8, stride=8), :]
                coef[8 * j + z, x : x + 8, :] = speed

    source = meta[3 * shots + 16]
    source_z = source // 16384 - 32 * half
    source_x = (source // 128) % 128 - 32 * quarter
    source_in = (source_z >= 0) & (source_z < 32) & (source_x >= 0) & (source_x < 32)
    source_at = jnp.where(source_in, (source_z * 32 + source_x) * 128 + source % 128, -1)
    spot = (
        lax.broadcasted_iota(jnp.int32, (4, 8, 128), 0) * 4096
        + lax.broadcasted_iota(jnp.int32, (4, 8, 128), 1) * 128
        + lax.broadcasted_iota(jnp.int32, (4, 8, 128), 2)
    )

    def laplacian(buf, n, z, xg):
        row = 8 + 8 * xg
        column = buf[n, pl.ds(z, 12), row : row + 8, :]
        total = lap[pl.ds(z, 4), 8 * xg : 8 * xg + 8, :]
        for k in range(1, 5):
            beside = column[4 + k : 8 + k] + column[4 - k : 8 - k]
            beside = beside + (
                buf[n, pl.ds(z + 4, 4), row + k : row + k + 8, :]
                + buf[n, pl.ds(z + 4, 4), row - k : row - k + 8, :]
            )
            total = total + COEF[k] * beside
        return column[4:8], total

    def ahead(n, z, xg):
        at = (pl.ds(z, 4), slice(8 * xg, 8 * xg + 8), slice(None))
        inner = (pl.ds(z + 4, 4), slice(8 + 8 * xg, 16 + 8 * xg), slice(None))
        here, total = laplacian(fwd, n + 1, z, xg)
        fired = jnp.where(spot == source_at - (z * 4096 + xg * 1024), wav[0, n], 0.0)
        speed = coef[at]
        change = (STEP_SQUARE * speed * speed) * (total + fired)
        upd[(n,) + at] = change
        new = 2.0 * here - fwd[(n,) + inner] + change
        fwd[(n + 2,) + inner] = new
        inj[(n,) + at] = count[at] * new - inj[(n,) + at]

    def back(t, z, xg):
        n = 5 - t
        at = (pl.ds(z, 4), slice(8 * xg, 8 * xg + 8), slice(None))
        inner = (pl.ds(z + 4, 4), slice(8 + 8 * xg, 16 + 8 * xg), slice(None))
        here, total = laplacian(adj, n + 1, z, xg)
        speed = coef[at]
        new = (
            2.0 * here
            - adj[(n + 2,) + inner]
            + (STEP_SQUARE * speed * speed) * (total + inj[(n,) + at])
        )
        adj[(n,) + inner] = new
        image[at] = image[at] + new * upd[(n,) + at]

    def group_at(i):
        return 4 * (i * half + (7 - i) * (1 - half))

    def march(buf, unit, t, now, new, e):
        more = t < STEPS - 1

        @pl.loop(1, 8)
        def _(i):
            for xg in (1, 2):
                unit(t, group_at(i), xg)

        z_copy(buf, now, e).wait_recv()
        x_take(buf, now, e, chunk_at(0))
        for xg in range(4):
            unit(t, group_at(0), xg)

        @pl.when(more)
        def _():
            z_copy(buf, new, e + 1).start()

        for xg in (0, 3):
            unit(t, group_at(1), xg)

        @pl.when(more)
        def _():
            x_post(buf, new, e + 1, chunk_at(0))

        @pl.loop(1, 4)
        def _(i):
            x_take(buf, now, e, chunk_at(i))
            for g in range(2):
                for xg in (0, 3):
                    unit(t, group_at(2 * i + g), xg)

            @pl.when(more)
            def _():
                x_post(buf, new, e + 1, chunk_at(i))

        @pl.when(more)
        def _():
            lateral(buf, new)

    @pl.loop(0, STEPS)
    def _(t):
        march(fwd, ahead, t, t + 1, t + 2, t)

    lateral(adj, 6)
    image[...] = jnp.zeros(image.shape, F32)

    @pl.loop(0, STEPS)
    def _(t):
        march(adj, back, t, 6 - t, 5 - t, 6 + t)

    @pl.loop(0, 8)
    def _(g):
        at = pl.ds(4 * g, 4)
        turn[pl.ds(128 * g, 128), :] = (2.0 * image[at] / coef[at]).reshape(128, 128)

    @pl.loop(0, 4)
    def _(j):
        for a in range(8):
            rows = [turn[pl.ds(256 * j + 4 * a + b, 8, stride=32), :] for b in range(4)]
            for ky in range(4):
                joined = None
                for b in range(4):
                    shift = (32 * (b - ky)) % 128
                    moved = pltpu.roll(rows[b], shift, 1) if shift else rows[b]
                    joined = moved if joined is None else jnp.where(lane_block == b, moved, joined)
                gtile[j, ky, :, 128 * a : 128 * a + 128] = joined

    def piece_copy(i):
        other = (slab + i) % 4
        return pltpu.make_async_remote_copy(
            src_ref=gtile.at[other],
            dst_ref=gpiece.at[pl.ds(4 * quarter, 4)],
            send_sem=p_send.at[i - 1],
            recv_sem=p_recv.at[i - 1],
            device_id={"ap": 4 * half + other},
            device_id_type=MESH,
        )

    for i in range(1, 4):
        piece_copy(i).start()
    gpiece[pl.ds(4 * quarter, 4)] = gtile[slab]
    for i in range(1, 4):
        piece_copy(i).wait_recv()

    @pl.loop(0, shots)
    def _(s):
        gsend[s] = gpiece[meta[2 * shots + 16 + s]]

    grecv[me] = gpiece[meta[2 * shots + 16 + me]]
    exchange_start(gsend, grecv, g_send, g_recv)

    out[...] = jnp.zeros(out.shape, F32)

    @pl.loop(0, shots // 8)
    def _(b):
        for i in range(8):
            s = 8 * b + i

            @pl.when(s != me)
            def _():
                arrival(gsend, grecv, s, g_send, g_recv).wait_recv()

        local = [meta[shots + 8 * b + i] for i in range(8)]

        for a in range(8):
            at = (slice(None), slice(128 * a, 128 * a + 128))
            parts = [grecv[(8 * b + i,) + at] for i in range(8)]
            for tile in range(16):
                total = out[(tile,) + at]
                for i in range(8):
                    total = total + jnp.where(local[i] == tile, 1.0, 0.0) * parts[i]
                out[(tile,) + at] = total

    for f in range(4):
        for i in range(1, 4):
            field_copy(f, i).wait_send()

    @pl.loop(0, shots)
    def _(s):
        @pl.when(s != me)
        def _():
            arrival(vsend, vrecv, s, v_send, v_recv).wait_send()
            arrival(gsend, grecv, s, g_send, g_recv).wait_send()

    for i in range(1, 4):
        tile_copy(i).wait_send()
        piece_copy(i).wait_send()

    @pl.loop(0, 2 * STEPS)
    def _(e):
        z_copy(fwd, 1, e).wait_send()

        @pl.loop(0, 4)
        def _(c):
            @pl.when(has_low)
            def _():
                x_copy(e, 0, c).wait_send()

            @pl.when(has_high)
            def _():
                x_copy(e, 1, c).wait_send()


def on_device(
    velocity_tiles,
    aperture_tiles,
    source_cells,
    wavelet,
    receiver_cells,
    observed,
    field_early,
    field_late,
    adjoint_late,
    adjoint_later,
):
    shots = lax.axis_size("shot")
    me = lax.axis_index("shot")
    tiles_dev = velocity_tiles.shape[0]
    owners = aperture_tiles // tiles_dev
    matched = owners == me
    local = jnp.sum(jnp.where(matched, aperture_tiles % tiles_dev, 0), axis=1)
    local_or_none = jnp.where(jnp.any(matched, axis=1), local, -1)
    row = lax.broadcasted_iota(jnp.int32, owners.shape, 0)
    mine = jnp.sum(jnp.where(row == me, owners, 0), axis=0)
    position = jnp.sum(
        jnp.where(mine[None, :] == row, lax.broadcasted_iota(jnp.int32, owners.shape, 1), 0), axis=1
    )
    meta = jnp.concatenate([local, local_or_none, mine, position, source_cells])

    vmem = pl.BlockSpec(memory_space=pltpu.VMEM)
    smem = pl.BlockSpec(memory_space=pltpu.SMEM)
    anywhere = pl.BlockSpec(memory_space=pl.ANY)
    block = (32, 32, 128)
    dma = pltpu.SemaphoreType.DMA
    return pl.pallas_call(
        kernel,
        out_shape=jax.ShapeDtypeStruct(velocity_tiles.shape, F32),
        in_specs=[smem, smem, vmem, vmem, vmem, anywhere, anywhere, anywhere, anywhere],
        out_specs=vmem,
        scratch_shapes=[
            pltpu.VMEM((8, 40, 48, 128), F32),
            pltpu.VMEM((8, 40, 48, 128), F32),
            pltpu.VMEM((STEPS,) + block, F32),
            pltpu.VMEM((STEPS,) + block, F32),
            pltpu.VMEM(block, F32),
            pltpu.VMEM(block, F32),
            pltpu.VMEM(block, F32),
            pltpu.VMEM(block, F32),
            pltpu.VMEM((1024, 128), F32),
            pltpu.VMEM((256, 256), BF16),
            pltpu.VMEM((1024, 256), BF16),
            pltpu.VMEM((2 * STEPS, 2, 32, 4, 128), F32),
            pltpu.VMEM((2 * STEPS, 2, 32, 4, 128), F32),
            pltpu.VMEM((shots, 8, 1024), F32),
            pltpu.VMEM((shots, 8, 1024), F32),
            pltpu.VMEM((16, 8, 1024), F32),
            pltpu.VMEM((4, 4, 8, 1024), F32),
            pltpu.VMEM((4, 4, 8, 1024), F32),
            pltpu.VMEM((16, 8, 1024), F32),
            pltpu.VMEM((shots, 8, 1024), F32),
            pltpu.VMEM((shots, 8, 1024), F32),
            dma((4, 3)),
            dma((4, 3)),
            dma((4,)),
            dma((2 * STEPS,)),
            dma((2 * STEPS,)),
            dma((2 * STEPS, 2, 4)),
            dma((2 * STEPS, 2, 4)),
            dma((shots,)),
            dma((shots,)),
            dma((shots,)),
            dma((shots,)),
            dma((3,)),
            dma((3,)),
            dma((3,)),
            dma((3,)),
        ],
        compiler_params=pltpu.CompilerParams(
            collective_id=0, has_side_effects=True, vmem_limit_bytes=60 * 1024 * 1024
        ),
        name="inversion",
    )(
        meta,
        wavelet,
        receiver_cells,
        observed,
        velocity_tiles,
        field_early,
        field_late,
        adjoint_late,
        adjoint_later,
    )


def solution(mesh):
    placed = (
        P("shot", "ap", None),
        P(),
        P("shot"),
        P("shot", None),
        P("shot", None),
        P("shot", None, None),
        P("shot", "ap", None, None),
        P("shot", "ap", None, None),
        P("shot", "ap", None, None),
        P("shot", "ap", None, None),
    )
    return jax.shard_map(
        on_device, mesh=mesh, in_specs=placed, out_specs=P("shot", "ap", None), check_vma=False
    )
```

profile of v0, /device:TPU:1, one launch (start us, length us, event | category | flops | bytes accessed | tf_op | source)
XLA Modules:
  0.0 136.0 jit_solution(8697587040907810895)
XLA Ops:
  0.0 0.0 copy-start
  0.7 0.0 copy-done
  0.7 0.1 select_reduce_fusion.1
  0.8 0.0 copy-start.1
  0.9 0.1 select_reduce_fusion
  1.0 0.7 concatenate.3.meta
  1.6 0.0 copy-done.1
  1.6 0.6 copy.11.observed
  2.2 131.8 %inversion.1 = f32[16,8,1024]{2,1,0:T(8,128)} custom-call(s32[113]{0:T(128)} %concatenate.3.meta, f32[1,6]{1,0:T(1,128)} %wav.1, s32[1,256]{1,0:T(1,128)} %cells.1, f32[1,6,256]{2,1,0:T(8,128)} %copy.11.observed, f32[16,8,1024]{2,1,0:T(8,128)} %vel.1, f32[1,8,128,128]{3,2,1,0:T(8,128)} %early.1, f32[1,8,128,128]{3,2,1,0:T(8,128)} %late.1, ...), custom_call_target="tpu_custom_call" | custom-call | tf_op jit(solution)/shard_map/inversion/pallas_call | solution.py:564
  134.1 1.9 %copy.14 = f32[16,8,1024]{2,1,0:T(8,128)} copy(f32[16,8,1024]{2,1,0:T(8,128)} %inversion.1) | data formatting | bytes 1048576
  (3 shorter events, 0.0 us)
Async XLA Ops:
  0.0 0.7 copy-start
  0.8 0.8 copy-start.1
where the time goes:
time: 136 us
  Pallas kernels  132 us (97%)
  local copies, waits for them, and re-layouts  3.18 us (2%)
    pallas_call x1, Pallas kernels, on_device(): pl.pallas_call(kernel, out_shape=jax.ShapeDtypeStruct(velocity_tiles.shap...  132 us

commit v1 on v0

--- a/solution.py
+++ b/solution.py
@@ -13,6 +13,7 @@
 STEPS = 6
 F32 = jnp.float32
 BF16 = jnp.bfloat16
+FACE_ORDER = (1, 2, 0, 3)
 Z_ORDER = (4, 3, 5, 2, 6, 1, 7, 0)
 
 
@@ -29,12 +30,16 @@
 
 
 def kernel(
-    meta, wav, cells, observed, vel, early, late, a_late, a_later, out,
+    tile_sent, tile_kept, tile_owner, tile_place, source_cell, wav, cells, observed, vel, early, late, a_late, a_later, out,
     fwd, adj, upd, inj, coef, count, image, lap, turn, ymat, hot,
-    xs, xr, vsend, vrecv, vpiece, vtile, gtile, gpiece, gsend, grecv,
+    xs, xr, vsend, vrecv0, vrecv1, vpiece, vtile0, vtile1, gtile, gpiece0, gpiece1,
+    gsend, grecv0, grecv1,
     f_send, f_recv, f_loc, z_send, z_recv, x_send, x_recv,
     v_send, v_recv, g_send, g_recv, t_send, t_recv, p_send, p_recv,
 ):
+    vrecv, vtile, gpiece, grecv = (
+        (vrecv0, vrecv1), (vtile0, vtile1), (gpiece0, gpiece1), (grecv0, grecv1)
+    )
     shots = lax.axis_size("shot")
     me = lax.axis_index("shot")
     ap = lax.axis_index("ap")
@@ -47,12 +52,6 @@
     has_low = quarter > 0
     has_high = quarter < 3
 
-    @pl.loop(1, 7)
-    def _(n):
-        for buf in (fwd, adj):
-            buf[n, 0:4, 8:40, :] = jnp.zeros((4, 32, 128), F32)
-            buf[n, 36:40, 8:40, :] = jnp.zeros((4, 32, 128), F32)
-
     fields = ((late, fwd, 1), (early, fwd, 0), (a_late, adj, 6), (a_later, adj, 7))
 
     def own_copy(f):
@@ -75,15 +74,22 @@
             device_id_type=MESH,
         )
 
-    for f in range(4):
-        own_copy(f).start()
-
     barrier = pltpu.get_barrier_semaphore()
+
+    side = (me // 2) % 2
+    beside = ap + 1 - 2 * (ap % 2)
+
+    def crossed(shot):
+        return (shot // 2 + side) % 2
 
     @pl.loop(1, shots)
     def _(d):
+        other = (me + d) % shots
         pl.semaphore_signal(
-            barrier, inc=1, device_id={"shot": (me + d) % shots}, device_id_type=MESH
+            barrier,
+            inc=1,
+            device_id={"shot": other, "ap": ap + (beside - ap) * crossed(other)},
+            device_id_type=MESH,
         )
 
     for i in range(1, 4):
@@ -93,11 +99,15 @@
     partner = ap_of(1 - half, quarter)
     pl.semaphore_signal(barrier, inc=1, device_id={"ap": partner}, device_id_type=MESH)
 
+    for f in range(4):
+        own_copy(f).start()
+
     @pl.loop(0, shots)
     def _(s):
-        vsend[s] = vel[meta[s]]
-
-    vrecv[me] = vel[meta[me]]
+        vsend[s] = vel[tile_sent[s]]
+
+    for h in range(2):
+        vrecv[h][me] = vel[tile_sent[me], :, 512 * h : 512 * h + 512]
 
     pl.semaphore_wait(barrier, shots - 1 + 4)
 
@@ -105,41 +115,43 @@
         for i in range(1, 4):
             field_copy(f, i).start()
 
-    def exchange_copy(src, dst, target, send, recv):
-        return pltpu.make_async_remote_copy(
-            src_ref=src.at[target],
-            dst_ref=dst.at[me],
-            send_sem=send.at[target],
-            recv_sem=recv.at[me],
-            device_id={"shot": target},
-            device_id_type=MESH,
-        )
-
-    def arrival(src, dst, origin, send, recv):
-        return pltpu.make_async_remote_copy(
-            src_ref=src.at[origin],
-            dst_ref=dst.at[origin],
-            send_sem=send.at[origin],
-            recv_sem=recv.at[origin],
+    def part(h):
+        return pl.ds(512 * h, 512)
+
+    def exchange_copy(src, dst, target, cross, h, send, recv):
+        return pltpu.make_async_remote_copy(
+            src_ref=src.at[target, :, part(h)],
+            dst_ref=dst[h].at[me],
+            send_sem=send.at[target, h],
+            recv_sem=recv.at[me, h],
+            device_id={"shot": target, "ap": beside if cross else ap},
+            device_id_type=MESH,
+        )
+
+    def arrival(src, dst, origin, h, send, recv):
+        return pltpu.make_async_remote_copy(
+            src_ref=src.at[origin, :, part(h)],
+            dst_ref=dst[h].at[origin],
+            send_sem=send.at[origin, h],
+            recv_sem=recv.at[origin, h],
             device_id={"shot": origin},
             device_id_type=MESH,
         )
 
-    def exchange_start(src, dst, send, recv):
+    def exchange_start(src, dst, core, h, send, recv):
         planes = shots // 4
+        for dz in range(planes):
+            for dy in range(2):
+                step = Z_ORDER[dz] if planes == 8 else dz
+                target = ((me // 4 + step) % planes) * 4 + ((me // 2 + dy) % 2) * 2 + core
+
+                @pl.when(target != me)
+                def _():
+                    exchange_copy(src, dst, target, dy, h, send, recv).start()
+
+    for h in range(2):
         for core in range(2):
-            for dz in range(planes):
-                for dy in range(2):
-                    step = Z_ORDER[dz] if planes == 8 else dz
-                    target = (
-                        ((me // 4 + step) % planes) * 4 + ((me // 2 + dy) % 2) * 2 + core
-                    )
-
-                    @pl.when(target != me)
-                    def _():
-                        exchange_copy(src, dst, target, send, recv).start()
-
-    exchange_start(vsend, vrecv, v_send, v_recv)
+            exchange_start(vsend, vrecv, core, h, v_send, v_recv)
 
     for f in (2, 3):
         for i in range(1, 4):
@@ -160,6 +172,9 @@
 
     @pl.loop(1, 7)
     def _(n):
+        for buf in (fwd, adj):
+            buf[n, pl.ds(36 * half, 4), 8:40, :] = jnp.zeros((4, 32, 128), F32)
+
         @pl.loop(0, 8)
         def _(g):
             for buf in (fwd, adj):
@@ -205,12 +220,12 @@
                 8, 32, 128
             )
 
-    def z_copy(buf, n, e):
-        return pltpu.make_async_remote_copy(
-            src_ref=buf.at[n, pl.ds(32 - 28 * half, 4), pl.ds(8, 32), :],
-            dst_ref=buf.at[n, pl.ds(36 * half, 4), pl.ds(8, 32), :],
-            send_sem=z_send.at[e],
-            recv_sem=z_recv.at[e],
+    def z_copy(buf, n, e, xg):
+        return pltpu.make_async_remote_copy(
+            src_ref=buf.at[n, pl.ds(32 - 28 * half, 4), pl.ds(8 + 8 * xg, 8), :],
+            dst_ref=buf.at[n, pl.ds(36 * half, 4), pl.ds(8 + 8 * xg, 8), :],
+            send_sem=z_send.at[e, xg],
+            recv_sem=z_recv.at[e, xg],
             device_id={"ap": partner},
             device_id_type=MESH,
         )
@@ -279,62 +294,77 @@
             found = jnp.dot(both, ymat[...], preferred_element_type=F32)
             lap[pl.ds(8 * c, 8), :, :] = (found[:, 0:128] + found[:, 128:256]).reshape(8, 32, 128)
 
-    for f, e in ((0, 0), (2, 6)):
+    def first_post(f, e):
         buf, n = fields[f][1:]
         fields_ready(f)
-        z_copy(buf, n, e).start()
+        for xg in FACE_ORDER:
+            z_copy(buf, n, e, xg).start()
         for i in range(4):
             x_post(buf, n, e, chunk_at(i))
+
+    first_post(0, 0)
     fields_ready(1)
-    fields_ready(3)
     lateral(fwd, 1)
 
-    @pl.loop(0, shots)
-    def _(s):
-        @pl.when(s != me)
-        def _():
-            arrival(vsend, vrecv, s, v_send, v_recv).wait_recv()
-
-    @pl.loop(0, 16)
-    def _(k):
-        vpiece[k] = vrecv[meta[2 * shots + k]]
-
-    def tile_copy(i):
+    def tile_copy(i, h):
         other = (quarter + i) % 4
         return pltpu.make_async_remote_copy(
-            src_ref=vpiece.at[pl.ds(4 * other, 4)],
-            dst_ref=vtile.at[slab],
-            send_sem=t_send.at[i - 1],
-            recv_sem=t_recv.at[i - 1],
+            src_ref=vpiece.at[pl.ds(4 * other, 4), :, part(h)],
+            dst_ref=vtile[h].at[slab],
+            send_sem=t_send.at[i - 1, h],
+            recv_sem=t_recv.at[i - 1, h],
             device_id={"ap": ap_of(half, other)},
             device_id_type=MESH,
         )
 
-    for i in range(1, 4):
-        tile_copy(i).start()
-    vtile[slab] = vpiece[pl.ds(4 * quarter, 4)]
-    for i in range(1, 4):
-        tile_copy(i).wait_recv()
+    turned = [crossed(tile_owner[4 * quarter + ky]) for ky in range(4)]
+    def at_slab(j, ky):
+        return j + turned[ky] * (1 - 2 * (j % 2))
 
     lane_block = lax.broadcasted_iota(jnp.int32, (8, 128), 1) // 32
 
-    @pl.loop(0, 4)
-    def _(j):
-        for a in range(8):
-            tiles = [vtile[j, ky, :, 128 * a : 128 * a + 128] for ky in range(4)]
-            for b in range(4):
-                joined = None
-                for ky in range(4):
-                    shift = (32 * (ky - b)) % 128
-                    moved = pltpu.roll(tiles[ky], shift, 1) if shift else tiles[ky]
-                    joined = moved if joined is None else jnp.where(lane_block == ky, moved, joined)
-                turn[8 * (4 * a + b) : 8 * (4 * a + b) + 8, :] = joined
-        for z in range(8):
-            for x in range(0, 32, 8):
-                speed = turn[pl.ds(8 * x + z, 8, stride=8), :]
-                coef[8 * j + z, x : x + 8, :] = speed
-
-    source = meta[3 * shots + 16]
+    for h in range(2):
+        lanes_h = slice(512 * h, 512 * h + 512)
+
+        @pl.loop(0, shots)
+        def _(s):
+            @pl.when(s != me)
+            def _():
+                arrival(vsend, vrecv, s, h, v_send, v_recv).wait_recv()
+
+        @pl.loop(0, 16)
+        def _(k):
+            vpiece[k, :, lanes_h] = vrecv[h][tile_owner[k]]
+
+        for i in range(1, 4):
+            tile_copy(i, h).start()
+        vtile[h][slab] = vpiece[pl.ds(4 * quarter, 4), :, lanes_h]
+
+    for h in range(2):
+        for i in range(1, 4):
+            tile_copy(i, h).wait_recv()
+
+        @pl.loop(0, 4)
+        def _(j):
+            for a in range(4 * h, 4 * h + 4):
+                tiles = [
+                    vtile[h][at_slab(j, ky), ky, :, 128 * (a % 4) : 128 * (a % 4) + 128]
+                    for ky in range(4)
+                ]
+                for b in range(4):
+                    joined = None
+                    for ky in range(4):
+                        shift = (32 * (ky - b)) % 128
+                        moved = pltpu.roll(tiles[ky], shift, 1) if shift else tiles[ky]
+                        joined = (
+                            moved if joined is None else jnp.where(lane_block == ky, moved, joined)
+                        )
+                    turn[8 * (4 * a + b) : 8 * (4 * a + b) + 8, :] = joined
+            for z in range(8):
+                for x in (16 * h, 16 * h + 8):
+                    coef[8 * j + z, x : x + 8, :] = turn[pl.ds(8 * x + z, 8, stride=8), :]
+
+    source = source_cell[0]
     source_z = source // 16384 - 32 * half
     source_x = (source // 128) % 128 - 32 * quarter
     source_in = (source_z >= 0) & (source_z < 32) & (source_x >= 0) & (source_x < 32)
@@ -395,14 +425,15 @@
             for xg in (1, 2):
                 unit(t, group_at(i), xg)
 
-        z_copy(buf, now, e).wait_recv()
-        x_take(buf, now, e, chunk_at(0))
-        for xg in range(4):
+        for xg in FACE_ORDER:
+            if xg == 0:
+                x_take(buf, now, e, chunk_at(0))
+            z_copy(buf, now, e, xg).wait_recv()
             unit(t, group_at(0), xg)
 
-        @pl.when(more)
-        def _():
-            z_copy(buf, new, e + 1).start()
+            @pl.when(more)
+            def _():
+                z_copy(buf, new, e + 1, xg).start()
 
         for xg in (0, 3):
             unit(t, group_at(1), xg)
@@ -430,6 +461,11 @@
     def _(t):
         march(fwd, ahead, t, t + 1, t + 2, t)
 
+        @pl.when(t == 3)
+        def _():
+            first_post(2, 6)
+
+    fields_ready(3)
     lateral(adj, 6)
     image[...] = jnp.zeros(image.shape, F32)
 
@@ -440,65 +476,78 @@
     @pl.loop(0, 8)
     def _(g):
         at = pl.ds(4 * g, 4)
-        turn[pl.ds(128 * g, 128), :] = (2.0 * image[at] / coef[at]).reshape(128, 128)
-
-    @pl.loop(0, 4)
-    def _(j):
-        for a in range(8):
-            rows = [turn[pl.ds(256 * j + 4 * a + b, 8, stride=32), :] for b in range(4)]
-            for ky in range(4):
-                joined = None
-                for b in range(4):
-                    shift = (32 * (b - ky)) % 128
-                    moved = pltpu.roll(rows[b], shift, 1) if shift else rows[b]
-                    joined = moved if joined is None else jnp.where(lane_block == b, moved, joined)
-                gtile[j, ky, :, 128 * a : 128 * a + 128] = joined
-
-    def piece_copy(i):
+        turn[pl.ds(128 * g, 128), :] = (image[at] / coef[at]).reshape(128, 128)
+
+    def piece_copy(i, h):
         other = (slab + i) % 4
         return pltpu.make_async_remote_copy(
-            src_ref=gtile.at[other],
-            dst_ref=gpiece.at[pl.ds(4 * quarter, 4)],
-            send_sem=p_send.at[i - 1],
-            recv_sem=p_recv.at[i - 1],
+            src_ref=gtile.at[other, :, :, part(h)],
+            dst_ref=gpiece[h].at[pl.ds(4 * quarter, 4)],
+            send_sem=p_send.at[i - 1, h],
+            recv_sem=p_recv.at[i - 1, h],
             device_id={"ap": 4 * half + other},
             device_id_type=MESH,
         )
 
-    for i in range(1, 4):
-        piece_copy(i).start()
-    gpiece[pl.ds(4 * quarter, 4)] = gtile[slab]
-    for i in range(1, 4):
-        piece_copy(i).wait_recv()
-
-    @pl.loop(0, shots)
-    def _(s):
-        gsend[s] = gpiece[meta[2 * shots + 16 + s]]
-
-    grecv[me] = gpiece[meta[2 * shots + 16 + me]]
-    exchange_start(gsend, grecv, g_send, g_recv)
+    for h in range(2):
+        lanes_h = slice(512 * h, 512 * h + 512)
+
+        @pl.loop(0, 4)
+        def _(j):
+            for a in range(4 * h, 4 * h + 4):
+                for ky in range(4):
+                    base = 256 * at_slab(j, ky) + 4 * a
+                    rows = [turn[pl.ds(base + b, 8, stride=32), :] for b in range(4)]
+                    joined = None
+                    for b in range(4):
+                        shift = (32 * (b - ky)) % 128
+                        moved = pltpu.roll(rows[b], shift, 1) if shift else rows[b]
+                        joined = (
+                            moved if joined is None else jnp.where(lane_block == b, moved, joined)
+                        )
+                    gtile[j, ky, :, 128 * a : 128 * a + 128] = joined
+
+        for i in range(1, 4):
+            piece_copy(i, h).start()
+        gpiece[h][pl.ds(4 * quarter, 4)] = gtile[slab, :, :, lanes_h]
+
+    for h in range(2):
+        lanes_h = slice(512 * h, 512 * h + 512)
+        for i in range(1, 4):
+            piece_copy(i, h).wait_recv()
+
+        @pl.loop(0, shots)
+        def _(s):
+            gsend[s, :, lanes_h] = gpiece[h][tile_place[s]]
+
+        grecv[h][me] = gpiece[h][tile_place[me]]
+        for core in range(2):
+            exchange_start(gsend, grecv, core, h, g_send, g_recv)
 
     out[...] = jnp.zeros(out.shape, F32)
 
-    @pl.loop(0, shots // 8)
-    def _(b):
-        for i in range(8):
-            s = 8 * b + i
-
-            @pl.when(s != me)
-            def _():
-                arrival(gsend, grecv, s, g_send, g_recv).wait_recv()
-
-        local = [meta[shots + 8 * b + i] for i in range(8)]
-
-        for a in range(8):
-            at = (slice(None), slice(128 * a, 128 * a + 128))
-            parts = [grecv[(8 * b + i,) + at] for i in range(8)]
-            for tile in range(16):
-                total = out[(tile,) + at]
-                for i in range(8):
-                    total = total + jnp.where(local[i] == tile, 1.0, 0.0) * parts[i]
-                out[(tile,) + at] = total
+    for h in range(2):
+
+        @pl.loop(0, shots // 8)
+        def _(b):
+            for i in range(8):
+                s = 8 * b + i
+
+                @pl.when(s != me)
+                def _():
+                    arrival(gsend, grecv, s, h, g_send, g_recv).wait_recv()
+
+            local = [tile_kept[8 * b + i] for i in range(8)]
+
+            for a in range(4 * h, 4 * h + 4):
+                at = (slice(None), slice(128 * a, 128 * a + 128))
+                here = (slice(None), slice(128 * (a % 4), 128 * (a % 4) + 128))
+                parts = [grecv[h][(8 * b + i,) + here] for i in range(8)]
+                for tile in range(16):
+                    total = out[(tile,) + at]
+                    for i in range(8):
+                        total = total + jnp.where(local[i] == tile, 1.0, 0.0) * parts[i]
+                    out[(tile,) + at] = total
 
     for f in range(4):
         for i in range(1, 4):
@@ -508,16 +557,19 @@
     def _(s):
         @pl.when(s != me)
         def _():
-            arrival(vsend, vrecv, s, v_send, v_recv).wait_send()
-            arrival(gsend, grecv, s, g_send, g_recv).wait_send()
-
-    for i in range(1, 4):
-        tile_copy(i).wait_send()
-        piece_copy(i).wait_send()
+            for h in range(2):
+                arrival(vsend, vrecv, s, h, v_send, v_recv).wait_send()
+                arrival(gsend, grecv, s, h, g_send, g_recv).wait_send()
+
+    for h in range(2):
+        for i in range(1, 4):
+            tile_copy(i, h).wait_send()
+            piece_copy(i, h).wait_send()
 
     @pl.loop(0, 2 * STEPS)
     def _(e):
-        z_copy(fwd, 1, e).wait_send()
+        for xg in range(4):
+            z_copy(fwd, 1, e, xg).wait_send()
 
         @pl.loop(0, 4)
         def _(c):
@@ -554,17 +606,16 @@
     position = jnp.sum(
         jnp.where(mine[None, :] == row, lax.broadcasted_iota(jnp.int32, owners.shape, 1), 0), axis=1
     )
-    meta = jnp.concatenate([local, local_or_none, mine, position, source_cells])
 
     vmem = pl.BlockSpec(memory_space=pltpu.VMEM)
     smem = pl.BlockSpec(memory_space=pltpu.SMEM)
     anywhere = pl.BlockSpec(memory_space=pl.ANY)
     block = (32, 32, 128)
     dma = pltpu.SemaphoreType.DMA
-    return pl.pallas_call(
+    half_gradient = pl.pallas_call(
         kernel,
         out_shape=jax.ShapeDtypeStruct(velocity_tiles.shape, F32),
-        in_specs=[smem, smem, vmem, vmem, vmem, anywhere, anywhere, anywhere, anywhere],
+        in_specs=[smem] * 6 + [vmem, vmem, vmem, anywhere, anywhere, anywhere, anywhere],
         out_specs=vmem,
         scratch_shapes=[
             pltpu.VMEM((8, 40, 48, 128), F32),
@@ -581,35 +632,43 @@
             pltpu.VMEM((2 * STEPS, 2, 32, 4, 128), F32),
             pltpu.VMEM((2 * STEPS, 2, 32, 4, 128), F32),
             pltpu.VMEM((shots, 8, 1024), F32),
+            pltpu.VMEM((shots, 8, 512), F32),
+            pltpu.VMEM((shots, 8, 512), F32),
+            pltpu.VMEM((16, 8, 1024), F32),
+            pltpu.VMEM((4, 4, 8, 512), F32),
+            pltpu.VMEM((4, 4, 8, 512), F32),
+            pltpu.VMEM((4, 4, 8, 1024), F32),
+            pltpu.VMEM((16, 8, 512), F32),
+            pltpu.VMEM((16, 8, 512), F32),
             pltpu.VMEM((shots, 8, 1024), F32),
-            pltpu.VMEM((16, 8, 1024), F32),
-            pltpu.VMEM((4, 4, 8, 1024), F32),
-            pltpu.VMEM((4, 4, 8, 1024), F32),
-            pltpu.VMEM((16, 8, 1024), F32),
-            pltpu.VMEM((shots, 8, 1024), F32),
-            pltpu.VMEM((shots, 8, 1024), F32),
+            pltpu.VMEM((shots, 8, 512), F32),
+            pltpu.VMEM((shots, 8, 512), F32),
             dma((4, 3)),
             dma((4, 3)),
             dma((4,)),
-            dma((2 * STEPS,)),
-            dma((2 * STEPS,)),
+            dma((2 * STEPS, 4)),
+            dma((2 * STEPS, 4)),
             dma((2 * STEPS, 2, 4)),
             dma((2 * STEPS, 2, 4)),
-            dma((shots,)),
-            dma((shots,)),
-            dma((shots,)),
-            dma((shots,)),
-            dma((3,)),
-            dma((3,)),
-            dma((3,)),
-            dma((3,)),
+            dma((shots, 2)),
+            dma((shots, 2)),
+            dma((shots, 2)),
+            dma((shots, 2)),
+            dma((3, 2)),
+            dma((3, 2)),
+            dma((3, 2)),
+            dma((3, 2)),
         ],
         compiler_params=pltpu.CompilerParams(
             collective_id=0, has_side_effects=True, vmem_limit_bytes=60 * 1024 * 1024
         ),
         name="inversion",
     )(
-        meta,
+        local,
+        local_or_none,
+        mine,
+        position,
+        source_cells,
         wavelet,
         receiver_cells,
         observed,
@@ -619,6 +678,7 @@
         adjoint_late,
         adjoint_later,
     )
+    return 2.0 * half_gradient
 
 
 def solution(mesh):

time: 136 us -> 119 us (0.88)
  Pallas kernels: 132 us -> 114 us
  other arithmetic: 0.25 us -> 3.17 us
  local copies, waits for them, and re-layouts: 3.18 us -> 1.2 us
    pallas_call x1, Pallas kernels: 132 us -> 114 us  [on_device(): pl.pallas_call(kernel, out_shape=jax.ShapeDtypeStruct(velocity_tiles.shap...]
    mul x0 -> x1, other arithmetic: none -> 1.88 us  [on_device(): return 2.0 * half_gradient]
where the time goes in v1:
time: 119 us
  Pallas kernels  114 us (96%)
  other arithmetic  3.17 us (3%)
  local copies, waits for them, and re-layouts  1.2 us (1%)
    pallas_call x1, Pallas kernels, on_device(): pl.pallas_call(kernel, out_shape=jax.ShapeDtypeStruct(velocity_tiles.shap...  114 us

profile of v1, /device:TPU:1, one launch (start us, length us, event | category | flops | bytes accessed | tf_op | source)
XLA Modules:
  0.0 119.0 jit_solution(17640032475754876011)
XLA Ops:
  0.0 0.0 copy-start
  0.7 0.0 copy-done
  0.7 0.1 select_reduce_fusion.1
  0.8 0.0 copy-start.3
  0.9 0.0 copy-start.2
  0.9 0.0 copy-start.1
  0.9 0.6 copy-done.3
  1.4 0.5 broadcast_select_fusion.tile_kept
  1.9 0.0 copy-done.2
  2.0 0.6 select_reduce_fusion.tile_place
  2.6 0.0 copy-done.1
  2.6 0.6 copy.11.observed
  3.2 114.0 %inversion.1 = f32[16,8,1024]{2,1,0:T(8,128)} custom-call(s32[32]{0:T(128)} %copy-done.3, s32[32]{0:T(128)} %broadcast_select_fusion.tile_kept, s32[16]{0:T(128)} %copy-done.2, s32[32]{0:T(128)} %select_reduce_fusion.tile_place, s32[1]{0:T(128)S(6)} %copy.12.source_cell, f32[1,6]{1,0:T(1,128)} %wav.1, s32[1,256]{1,0:T(1,128)} %cells.1, ...), custom_call_target="tpu_custom_call" | custom-call | tf_op jit(solution)/shard_map/inversion/pallas_call | solution.py:615
  117.2 1.9 %broadcast_multiply_fusion = f32[16,8,1024]{2,1,0:T(8,128)} fusion(f32[16,8,1024]{2,1,0:T(8,128)} %inversion.1), kind=kLoop, calls=%fused_computation | loop fusion | flops 131072 | bytes 1048576 | tf_op jit(solution)/shard_map/mul | solution.py:681
  (2 shorter events, 0.0 us)
Async XLA Ops:
  0.0 0.7 copy-start
  0.8 0.6 copy-start.3
  0.9 1.1 copy-start.2
  0.9 1.7 %copy-start.1 = (f32[1,6,256]{2,0,1:T(1,128)S(1)}, f32[1,6,256]{2,0,1:T(1,128)}, u32[]{:S(2)}) copy-start(f32[1,6,256]{2,0,1:T(1,128)} %param.15) | copy-start | bytes 18436

commit v2 on v1

--- a/solution.py
+++ b/solution.py
@@ -13,6 +13,9 @@
 STEPS = 6
 F32 = jnp.float32
 BF16 = jnp.bfloat16
+PARTS = 2
+BLOCKS = 8 // PARTS
+WIDE = 128 * BLOCKS
 FACE_ORDER = (1, 2, 0, 3)
 Z_ORDER = (4, 3, 5, 2, 6, 1, 7, 0)
 
@@ -30,16 +33,12 @@
 
 
 def kernel(
-    tile_sent, tile_kept, tile_owner, tile_place, source_cell, wav, cells, observed, vel, early, late, a_late, a_later, out,
+    table, wav, cells, observed_at, vel_at, early, late, a_late, a_later, out,
     fwd, adj, upd, inj, coef, count, image, lap, turn, ymat, hot,
-    xs, xr, vsend, vrecv0, vrecv1, vpiece, vtile0, vtile1, gtile, gpiece0, gpiece1,
-    gsend, grecv0, grecv1,
-    f_send, f_recv, f_loc, z_send, z_recv, x_send, x_recv,
+    xs, xr, vsend, vrecv, vpiece, vtile, gtile, gpiece, gsend, grecv, vel, observed,
+    i_sem, f_send, f_recv, f_loc, z_send, z_recv, x_send, x_recv,
     v_send, v_recv, g_send, g_recv, t_send, t_recv, p_send, p_recv,
 ):
-    vrecv, vtile, gpiece, grecv = (
-        (vrecv0, vrecv1), (vtile0, vtile1), (gpiece0, gpiece1), (grecv0, grecv1)
-    )
     shots = lax.axis_size("shot")
     me = lax.axis_index("shot")
     ap = lax.axis_index("ap")
@@ -74,6 +73,9 @@
             device_id_type=MESH,
         )
 
+    vel_copy = pltpu.make_async_copy(vel_at, vel, i_sem.at[0])
+    observed_copy = pltpu.make_async_copy(observed_at.at[0], observed, i_sem.at[1])
+    vel_copy.start()
     barrier = pltpu.get_barrier_semaphore()
 
     side = (me // 2) % 2
@@ -101,13 +103,15 @@
 
     for f in range(4):
         own_copy(f).start()
+    observed_copy.start()
+    vel_copy.wait()
 
     @pl.loop(0, shots)
     def _(s):
-        vsend[s] = vel[tile_sent[s]]
-
-    for h in range(2):
-        vrecv[h][me] = vel[tile_sent[me], :, 512 * h : 512 * h + 512]
+        vsend[s] = vel[table[s]]
+
+    for h in range(PARTS):
+        vrecv[h][me] = vel[table[me], :, WIDE * h : WIDE * h + WIDE]
 
     pl.semaphore_wait(barrier, shots - 1 + 4)
 
@@ -116,7 +120,7 @@
             field_copy(f, i).start()
 
     def part(h):
-        return pl.ds(512 * h, 512)
+        return pl.ds(WIDE * h, WIDE)
 
     def exchange_copy(src, dst, target, cross, h, send, recv):
         return pltpu.make_async_remote_copy(
@@ -149,7 +153,7 @@
                 def _():
                     exchange_copy(src, dst, target, dy, h, send, recv).start()
 
-    for h in range(2):
+    for h in range(PARTS):
         for core in range(2):
             exchange_start(vsend, vrecv, core, h, v_send, v_recv)
 
@@ -207,8 +211,9 @@
         )
         count[pl.ds(8 * b, 8), :, :] = found.reshape(8, 32, 128)
 
+    observed_copy.wait()
     for n in range(STEPS):
-        high, low = split(lanes * observed[0, n : n + 1, :])
+        high, low = split(lanes * observed[n : n + 1, :])
         both = jnp.concatenate([high, low], axis=0)
 
         @pl.loop(0, 4)
@@ -317,14 +322,14 @@
             device_id_type=MESH,
         )
 
-    turned = [crossed(tile_owner[4 * quarter + ky]) for ky in range(4)]
+    turned = [crossed(table[2 * shots + 4 * quarter + ky]) for ky in range(4)]
     def at_slab(j, ky):
         return j + turned[ky] * (1 - 2 * (j % 2))
 
     lane_block = lax.broadcasted_iota(jnp.int32, (8, 128), 1) // 32
 
-    for h in range(2):
-        lanes_h = slice(512 * h, 512 * h + 512)
+    for h in range(PARTS):
+        lanes_h = slice(WIDE * h, WIDE * h + WIDE)
 
         @pl.loop(0, shots)
         def _(s):
@@ -334,21 +339,21 @@
 
         @pl.loop(0, 16)
         def _(k):
-            vpiece[k, :, lanes_h] = vrecv[h][tile_owner[k]]
+            vpiece[k, :, lanes_h] = vrecv[h][table[2 * shots + k]]
 
         for i in range(1, 4):
             tile_copy(i, h).start()
         vtile[h][slab] = vpiece[pl.ds(4 * quarter, 4), :, lanes_h]
 
-    for h in range(2):
+    for h in range(PARTS):
         for i in range(1, 4):
             tile_copy(i, h).wait_recv()
 
         @pl.loop(0, 4)
         def _(j):
-            for a in range(4 * h, 4 * h + 4):
+            for a in range(BLOCKS * h, BLOCKS * h + BLOCKS):
                 tiles = [
-                    vtile[h][at_slab(j, ky), ky, :, 128 * (a % 4) : 128 * (a % 4) + 128]
+                    vtile[h][at_slab(j, ky), ky, :, 128 * (a % BLOCKS) : 128 * (a % BLOCKS) + 128]
                     for ky in range(4)
                 ]
                 for b in range(4):
@@ -361,10 +366,10 @@
                         )
                     turn[8 * (4 * a + b) : 8 * (4 * a + b) + 8, :] = joined
             for z in range(8):
-                for x in (16 * h, 16 * h + 8):
+                for x in range(4 * BLOCKS * h, 4 * BLOCKS * h + 4 * BLOCKS, 8):
                     coef[8 * j + z, x : x + 8, :] = turn[pl.ds(8 * x + z, 8, stride=8), :]
 
-    source = source_cell[0]
+    source = table[3 * shots + 16]
     source_z = source // 16384 - 32 * half
     source_x = (source // 128) % 128 - 32 * quarter
     source_in = (source_z >= 0) & (source_z < 32) & (source_x >= 0) & (source_x < 32)
@@ -489,12 +494,12 @@
             device_id_type=MESH,
         )
 
-    for h in range(2):
-        lanes_h = slice(512 * h, 512 * h + 512)
+    for h in range(PARTS):
+        lanes_h = slice(WIDE * h, WIDE * h + WIDE)
 
         @pl.loop(0, 4)
         def _(j):
-            for a in range(4 * h, 4 * h + 4):
+            for a in range(BLOCKS * h, BLOCKS * h + BLOCKS):
                 for ky in range(4):
                     base = 256 * at_slab(j, ky) + 4 * a
                     rows = [turn[pl.ds(base + b, 8, stride=32), :] for b in range(4)]
@@ -511,38 +516,43 @@
             piece_copy(i, h).start()
         gpiece[h][pl.ds(4 * quarter, 4)] = gtile[slab, :, :, lanes_h]
 
-    for h in range(2):
-        lanes_h = slice(512 * h, 512 * h + 512)
+    for h in range(PARTS):
+        lanes_h = slice(WIDE * h, WIDE * h + WIDE)
         for i in range(1, 4):
             piece_copy(i, h).wait_recv()
 
         @pl.loop(0, shots)
         def _(s):
-            gsend[s, :, lanes_h] = gpiece[h][tile_place[s]]
-
-        grecv[h][me] = gpiece[h][tile_place[me]]
+            gsend[s, :, lanes_h] = gpiece[h][table[2 * shots + 16 + s]]
+
+        grecv[h][me] = gpiece[h][table[2 * shots + 16 + me]]
         for core in range(2):
             exchange_start(gsend, grecv, core, h, g_send, g_recv)
 
     out[...] = jnp.zeros(out.shape, F32)
-
-    for h in range(2):
+    planes = shots // 4
+
+    def nearer(m):
+        away = planes // 2 - ((m + 1) // 2) * (2 * (m % 2) - 1)
+        return 4 * ((me // 4 + planes - away) % planes)
+
+    for h in range(PARTS):
 
         @pl.loop(0, shots // 8)
         def _(b):
-            for i in range(8):
-                s = 8 * b + i
+            origins = [nearer(2 * b + i // 4) + i % 4 for i in range(8)]
+            for s in origins:
 
                 @pl.when(s != me)
                 def _():
                     arrival(gsend, grecv, s, h, g_send, g_recv).wait_recv()
 
-            local = [tile_kept[8 * b + i] for i in range(8)]
-
-            for a in range(4 * h, 4 * h + 4):
+            local = [table[shots + s] for s in origins]
+
+            for a in range(BLOCKS * h, BLOCKS * h + BLOCKS):
                 at = (slice(None), slice(128 * a, 128 * a + 128))
-                here = (slice(None), slice(128 * (a % 4), 128 * (a % 4) + 128))
-                parts = [grecv[h][(8 * b + i,) + here] for i in range(8)]
+                here = (slice(None), slice(128 * (a % BLOCKS), 128 * (a % BLOCKS) + 128))
+                parts = [grecv[h][(s,) + here] for s in origins]
                 for tile in range(16):
                     total = out[(tile,) + at]
                     for i in range(8):
@@ -557,11 +567,11 @@
     def _(s):
         @pl.when(s != me)
         def _():
-            for h in range(2):
+            for h in range(PARTS):
                 arrival(vsend, vrecv, s, h, v_send, v_recv).wait_send()
                 arrival(gsend, grecv, s, h, g_send, g_recv).wait_send()
 
-    for h in range(2):
+    for h in range(PARTS):
         for i in range(1, 4):
             tile_copy(i, h).wait_send()
             piece_copy(i, h).wait_send()
@@ -615,7 +625,7 @@
     half_gradient = pl.pallas_call(
         kernel,
         out_shape=jax.ShapeDtypeStruct(velocity_tiles.shape, F32),
-        in_specs=[smem] * 6 + [vmem, vmem, vmem, anywhere, anywhere, anywhere, anywhere],
+        in_specs=[smem, smem, vmem, anywhere, anywhere, anywhere, anywhere, anywhere, anywhere],
         out_specs=vmem,
         scratch_shapes=[
             pltpu.VMEM((8, 40, 48, 128), F32),
@@ -632,17 +642,16 @@
             pltpu.VMEM((2 * STEPS, 2, 32, 4, 128), F32),
             pltpu.VMEM((2 * STEPS, 2, 32, 4, 128), F32),
             pltpu.VMEM((shots, 8, 1024), F32),
-            pltpu.VMEM((shots, 8, 512), F32),
-            pltpu.VMEM((shots, 8, 512), F32),
+            (pltpu.VMEM((shots, 8, WIDE), F32),) * PARTS,
             pltpu.VMEM((16, 8, 1024), F32),
-            pltpu.VMEM((4, 4, 8, 512), F32),
-            pltpu.VMEM((4, 4, 8, 512), F32),
+            (pltpu.VMEM((4, 4, 8, WIDE), F32),) * PARTS,
             pltpu.VMEM((4, 4, 8, 1024), F32),
-            pltpu.VMEM((16, 8, 512), F32),
-            pltpu.VMEM((16, 8, 512), F32),
+            (pltpu.VMEM((16, 8, WIDE), F32),) * PARTS,
             pltpu.VMEM((shots, 8, 1024), F32),
-            pltpu.VMEM((shots, 8, 512), F32),
-            pltpu.VMEM((shots, 8, 512), F32),
+            (pltpu.VMEM((shots, 8, WIDE), F32),) * PARTS,
+            pltpu.VMEM((16, 8, 1024), F32),
+            pltpu.VMEM((STEPS, 256), F32),
+            dma((2,)),
             dma((4, 3)),
             dma((4, 3)),
             dma((4,)),
@@ -650,25 +659,21 @@
             dma((2 * STEPS, 4)),
             dma((2 * STEPS, 2, 4)),
             dma((2 * STEPS, 2, 4)),
-            dma((shots, 2)),
-            dma((shots, 2)),
-            dma((shots, 2)),
-            dma((shots, 2)),
-            dma((3, 2)),
-            dma((3, 2)),
-            dma((3, 2)),
-            dma((3, 2)),
+            dma((shots, PARTS)),
+            dma((shots, PARTS)),
+            dma((shots, PARTS)),
+            dma((shots, PARTS)),
+            dma((3, PARTS)),
+            dma((3, PARTS)),
+            dma((3, PARTS)),
+            dma((3, PARTS)),
         ],
         compiler_params=pltpu.CompilerParams(
             collective_id=0, has_side_effects=True, vmem_limit_bytes=60 * 1024 * 1024
         ),
         name="inversion",
     )(
-        local,
-        local_or_none,
-        mine,
-        position,
-        source_cells,
+        jnp.concatenate([local, local_or_none, mine, position, source_cells]),
         wavelet,
         receiver_cells,
         observed,

time: 119 us -> 118 us (level)
  no operation moved by 1% of the time
where the time goes in v2:
time: 118 us
  Pallas kernels  114 us (97%)
  other arithmetic  2.14 us (2%)
  local copies, waits for them, and re-layouts  1.3 us (1%)
    pallas_call x1, Pallas kernels, on_device(): pl.pallas_call(kernel, out_shape=jax.ShapeDtypeStruct(velocity_tiles.shap...  114 us

profile of v2, /device:TPU:1, one launch (start us, length us, event | category | flops | bytes accessed | tf_op | source)
XLA Modules:
  0.0 117.8 jit_solution(2880194514708149220)
XLA Ops:
  0.0 0.0 copy-start
  0.7 0.0 copy-done
  0.7 0.1 select_reduce_fusion.1
  0.8 0.0 copy-start.1
  0.9 0.1 select_reduce_fusion
  1.0 0.7 concatenate.3.table
  1.6 0.0 copy-done.1
  1.6 0.6 copy.11.observed_at
  2.2 113.6 %inversion.1 = f32[16,8,1024]{2,1,0:T(8,128)} custom-call(s32[113]{0:T(128)} %concatenate.3.table, f32[1,6]{1,0:T(1,128)} %wav.1, s32[1,256]{1,0:T(1,128)} %cells.1, f32[1,6,256]{2,1,0:T(8,128)} %copy.11.observed_at, f32[16,8,1024]{2,1,0:T(8,128)} %vel_at.1, f32[1,8,128,128]{3,2,1,0:T(8,128)} %early.1, f32[1,8,128,128]{3,2,1,0:T(8,128)} %late.1, ...), custom_call_target="tpu_custom_call" | custom-call | tf_op jit(solution)/shard_map/inversion/pallas_call | solution.py:625
  115.9 1.9 %broadcast_multiply_fusion = f32[16,8,1024]{2,1,0:T(8,128)} fusion(f32[16,8,1024]{2,1,0:T(8,128)} %inversion.1), kind=kLoop, calls=%fused_computation | loop fusion | flops 131072 | bytes 1048576 | tf_op jit(solution)/shard_map/mul | solution.py:686
  (3 shorter events, 0.0 us)
Async XLA Ops:
  0.0 0.7 copy-start
  0.8 0.8 copy-start.1

commit v3 on v2

--- a/solution.py
+++ b/solution.py
@@ -14,8 +14,8 @@
 F32 = jnp.float32
 BF16 = jnp.bfloat16
 PARTS = 2
-BLOCKS = 8 // PARTS
-WIDE = 128 * BLOCKS
+VEL_CUTS = (0, 6, 8)
+GRAD_CUTS = (0, 2, 8)
 FACE_ORDER = (1, 2, 0, 3)
 Z_ORDER = (4, 3, 5, 2, 6, 1, 7, 0)
 
@@ -32,10 +32,18 @@
     return high, (value - high.astype(F32)).astype(BF16)
 
 
+def part(cuts, h):
+    return pl.ds(128 * cuts[h], 128 * (cuts[h + 1] - cuts[h]))
+
+
+def blocks(cuts, h):
+    return range(cuts[h], cuts[h + 1])
+
+
 def kernel(
-    table, wav, cells, observed_at, vel_at, early, late, a_late, a_later, out,
+    table, source_cell, wav, cells, observed, vel_at, early, late, a_late, a_later, out,
     fwd, adj, upd, inj, coef, count, image, lap, turn, ymat, hot,
-    xs, xr, vsend, vrecv, vpiece, vtile, gtile, gpiece, gsend, grecv, vel, observed,
+    xs, xr, vsend, vrecv, vpiece, vtile, gtile, gpiece, gsend, grecv, vel,
     i_sem, f_send, f_recv, f_loc, z_send, z_recv, x_send, x_recv,
     v_send, v_recv, g_send, g_recv, t_send, t_recv, p_send, p_recv,
 ):
@@ -74,7 +82,6 @@
         )
 
     vel_copy = pltpu.make_async_copy(vel_at, vel, i_sem.at[0])
-    observed_copy = pltpu.make_async_copy(observed_at.at[0], observed, i_sem.at[1])
     vel_copy.start()
     barrier = pltpu.get_barrier_semaphore()
 
@@ -103,15 +110,14 @@
 
     for f in range(4):
         own_copy(f).start()
-    observed_copy.start()
     vel_copy.wait()
 
     @pl.loop(0, shots)
     def _(s):
-        vsend[s] = vel[table[s]]
+        vsend[s] = vel[table[0, s]]
 
     for h in range(PARTS):
-        vrecv[h][me] = vel[table[me], :, WIDE * h : WIDE * h + WIDE]
+        vrecv[h][me] = vel[table[0, me], :, part(VEL_CUTS, h)]
 
     pl.semaphore_wait(barrier, shots - 1 + 4)
 
@@ -119,12 +125,12 @@
         for i in range(1, 4):
             field_copy(f, i).start()
 
-    def part(h):
-        return pl.ds(WIDE * h, WIDE)
+    def cuts_of(src):
+        return VEL_CUTS if src is vsend else GRAD_CUTS
 
     def exchange_copy(src, dst, target, cross, h, send, recv):
         return pltpu.make_async_remote_copy(
-            src_ref=src.at[target, :, part(h)],
+            src_ref=src.at[target, :, part(cuts_of(src), h)],
             dst_ref=dst[h].at[me],
             send_sem=send.at[target, h],
             recv_sem=recv.at[me, h],
@@ -134,7 +140,7 @@
 
     def arrival(src, dst, origin, h, send, recv):
         return pltpu.make_async_remote_copy(
-            src_ref=src.at[origin, :, part(h)],
+            src_ref=src.at[origin, :, part(cuts_of(src), h)],
             dst_ref=dst[h].at[origin],
             send_sem=send.at[origin, h],
             recv_sem=recv.at[origin, h],
@@ -211,9 +217,8 @@
         )
         count[pl.ds(8 * b, 8), :, :] = found.reshape(8, 32, 128)
 
-    observed_copy.wait()
     for n in range(STEPS):
-        high, low = split(lanes * observed[n : n + 1, :])
+        high, low = split(lanes * observed[0:1, nrec * n : nrec * n + nrec])
         both = jnp.concatenate([high, low], axis=0)
 
         @pl.loop(0, 4)
@@ -314,7 +319,7 @@
     def tile_copy(i, h):
         other = (quarter + i) % 4
         return pltpu.make_async_remote_copy(
-            src_ref=vpiece.at[pl.ds(4 * other, 4), :, part(h)],
+            src_ref=vpiece.at[pl.ds(4 * other, 4), :, part(VEL_CUTS, h)],
             dst_ref=vtile[h].at[slab],
             send_sem=t_send.at[i - 1, h],
             recv_sem=t_recv.at[i - 1, h],
@@ -322,14 +327,14 @@
             device_id_type=MESH,
         )
 
-    turned = [crossed(table[2 * shots + 4 * quarter + ky]) for ky in range(4)]
+    turned = [crossed(table[3, 4 * quarter + ky]) for ky in range(4)]
     def at_slab(j, ky):
         return j + turned[ky] * (1 - 2 * (j % 2))
 
     lane_block = lax.broadcasted_iota(jnp.int32, (8, 128), 1) // 32
 
     for h in range(PARTS):
-        lanes_h = slice(WIDE * h, WIDE * h + WIDE)
+        lanes_h = part(VEL_CUTS, h)
 
         @pl.loop(0, shots)
         def _(s):
@@ -339,7 +344,7 @@
 
         @pl.loop(0, 16)
         def _(k):
-            vpiece[k, :, lanes_h] = vrecv[h][table[2 * shots + k]]
+            vpiece[k, :, lanes_h] = vrecv[h][table[3, k]]
 
         for i in range(1, 4):
             tile_copy(i, h).start()
@@ -351,9 +356,9 @@
 
         @pl.loop(0, 4)
         def _(j):
-            for a in range(BLOCKS * h, BLOCKS * h + BLOCKS):
+            for a in blocks(VEL_CUTS, h):
                 tiles = [
-                    vtile[h][at_slab(j, ky), ky, :, 128 * (a % BLOCKS) : 128 * (a % BLOCKS) + 128]
+                    vtile[h][at_slab(j, ky), ky, :, 128 * (a - VEL_CUTS[h]) : 128 * (a - VEL_CUTS[h]) + 128]
                     for ky in range(4)
                 ]
                 for b in range(4):
@@ -366,10 +371,10 @@
                         )
                     turn[8 * (4 * a + b) : 8 * (4 * a + b) + 8, :] = joined
             for z in range(8):
-                for x in range(4 * BLOCKS * h, 4 * BLOCKS * h + 4 * BLOCKS, 8):
+                for x in range(4 * VEL_CUTS[h], 4 * VEL_CUTS[h + 1], 8):
                     coef[8 * j + z, x : x + 8, :] = turn[pl.ds(8 * x + z, 8, stride=8), :]
 
-    source = table[3 * shots + 16]
+    source = source_cell[0]
     source_z = source // 16384 - 32 * half
     source_x = (source // 128) % 128 - 32 * quarter
     source_in = (source_z >= 0) & (source_z < 32) & (source_x >= 0) & (source_x < 32)
@@ -486,7 +491,7 @@
     def piece_copy(i, h):
         other = (slab + i) % 4
         return pltpu.make_async_remote_copy(
-            src_ref=gtile.at[other, :, :, part(h)],
+            src_ref=gtile.at[other, :, :, part(GRAD_CUTS, h)],
             dst_ref=gpiece[h].at[pl.ds(4 * quarter, 4)],
             send_sem=p_send.at[i - 1, h],
             recv_sem=p_recv.at[i - 1, h],
@@ -495,11 +500,11 @@
         )
 
     for h in range(PARTS):
-        lanes_h = slice(WIDE * h, WIDE * h + WIDE)
+        lanes_h = part(GRAD_CUTS, h)
 
         @pl.loop(0, 4)
         def _(j):
-            for a in range(BLOCKS * h, BLOCKS * h + BLOCKS):
+            for a in blocks(GRAD_CUTS, h):
                 for ky in range(4):
                     base = 256 * at_slab(j, ky) + 4 * a
                     rows = [turn[pl.ds(base + b, 8, stride=32), :] for b in range(4)]
@@ -517,15 +522,15 @@
         gpiece[h][pl.ds(4 * quarter, 4)] = gtile[slab, :, :, lanes_h]
 
     for h in range(PARTS):
-        lanes_h = slice(WIDE * h, WIDE * h + WIDE)
+        lanes_h = part(GRAD_CUTS, h)
         for i in range(1, 4):
             piece_copy(i, h).wait_recv()
 
         @pl.loop(0, shots)
         def _(s):
-            gsend[s, :, lanes_h] = gpiece[h][table[2 * shots + 16 + s]]
-
-        grecv[h][me] = gpiece[h][table[2 * shots + 16 + me]]
+            gsend[s, :, lanes_h] = gpiece[h][table[2, s]]
+
+        grecv[h][me] = gpiece[h][table[2, me]]
         for core in range(2):
             exchange_start(gsend, grecv, core, h, g_send, g_recv)
 
@@ -547,11 +552,11 @@
                 def _():
                     arrival(gsend, grecv, s, h, g_send, g_recv).wait_recv()
 
-            local = [table[shots + s] for s in origins]
-
-            for a in range(BLOCKS * h, BLOCKS * h + BLOCKS):
+            local = [table[1, s] for s in origins]
+
+            for a in blocks(GRAD_CUTS, h):
                 at = (slice(None), slice(128 * a, 128 * a + 128))
-                here = (slice(None), slice(128 * (a % BLOCKS), 128 * (a % BLOCKS) + 128))
+                here = (slice(None), pl.ds(128 * (a - GRAD_CUTS[h]), 128))
                 parts = [grecv[h][(s,) + here] for s in origins]
                 for tile in range(16):
                     total = out[(tile,) + at]
@@ -607,15 +612,16 @@
     shots = lax.axis_size("shot")
     me = lax.axis_index("shot")
     tiles_dev = velocity_tiles.shape[0]
-    owners = aperture_tiles // tiles_dev
-    matched = owners == me
-    local = jnp.sum(jnp.where(matched, aperture_tiles % tiles_dev, 0), axis=1)
-    local_or_none = jnp.where(jnp.any(matched, axis=1), local, -1)
-    row = lax.broadcasted_iota(jnp.int32, owners.shape, 0)
-    mine = jnp.sum(jnp.where(row == me, owners, 0), axis=0)
-    position = jnp.sum(
-        jnp.where(mine[None, :] == row, lax.broadcasted_iota(jnp.int32, owners.shape, 1), 0), axis=1
-    )
+    extent = (4,) + aperture_tiles.shape
+    which, row, column = (lax.broadcasted_iota(jnp.int32, extent, d) for d in range(3))
+    owners = (aperture_tiles // tiles_dev)[None]
+    local = (aperture_tiles % tiles_dev)[None]
+    mine = lax.dynamic_slice_in_dim(owners, me, 1, 1)
+    taken = jnp.where(owners == me, local + jnp.minimum(which, 1), 0)
+    placed = jnp.where(mine == row, column, 0)
+    listed = jnp.where(column == row, mine, 0)
+    terms = jnp.where(which < 2, taken, jnp.where(which == 2, placed, listed))
+    table = jnp.sum(terms, axis=2) - jnp.where(which[:, :, 0] == 1, 1, 0)
 
     vmem = pl.BlockSpec(memory_space=pltpu.VMEM)
     smem = pl.BlockSpec(memory_space=pltpu.SMEM)
@@ -625,7 +631,7 @@
     half_gradient = pl.pallas_call(
         kernel,
         out_shape=jax.ShapeDtypeStruct(velocity_tiles.shape, F32),
-        in_specs=[smem, smem, vmem, anywhere, anywhere, anywhere, anywhere, anywhere, anywhere],
+        in_specs=[smem, smem, smem, vmem, vmem, anywhere, anywhere, anywhere, anywhere, anywhere],
         out_specs=vmem,
         scratch_shapes=[
             pltpu.VMEM((8, 40, 48, 128), F32),
@@ -642,16 +648,15 @@
             pltpu.VMEM((2 * STEPS, 2, 32, 4, 128), F32),
             pltpu.VMEM((2 * STEPS, 2, 32, 4, 128), F32),
             pltpu.VMEM((shots, 8, 1024), F32),
-            (pltpu.VMEM((shots, 8, WIDE), F32),) * PARTS,
+            tuple(pltpu.VMEM((shots, 8, 128 * (VEL_CUTS[h + 1] - VEL_CUTS[h])), F32) for h in range(PARTS)),
             pltpu.VMEM((16, 8, 1024), F32),
-            (pltpu.VMEM((4, 4, 8, WIDE), F32),) * PARTS,
+            tuple(pltpu.VMEM((4, 4, 8, 128 * (VEL_CUTS[h + 1] - VEL_CUTS[h])), F32) for h in range(PARTS)),
             pltpu.VMEM((4, 4, 8, 1024), F32),
-            (pltpu.VMEM((16, 8, WIDE), F32),) * PARTS,
+            tuple(pltpu.VMEM((16, 8, 128 * (GRAD_CUTS[h + 1] - GRAD_CUTS[h])), F32) for h in range(PARTS)),
             pltpu.VMEM((shots, 8, 1024), F32),
-            (pltpu.VMEM((shots, 8, WIDE), F32),) * PARTS,
+            tuple(pltpu.VMEM((shots, 8, 128 * (GRAD_CUTS[h + 1] - GRAD_CUTS[h])), F32) for h in range(PARTS)),
             pltpu.VMEM((16, 8, 1024), F32),
-            pltpu.VMEM((STEPS, 256), F32),
-            dma((2,)),
+            dma((1,)),
             dma((4, 3)),
             dma((4, 3)),
             dma((4,)),
@@ -673,10 +678,11 @@
         ),
         name="inversion",
     )(
-        jnp.concatenate([local, local_or_none, mine, position, source_cells]),
+        table,
+        source_cells,
         wavelet,
         receiver_cells,
-        observed,
+        observed.reshape(1, -1),
         velocity_tiles,
         field_early,
         field_late,

time: 118 us -> 116 us (0.983)
  Pallas kernels: 114 us -> 112 us
    pallas_call x1, Pallas kernels: 114 us -> 112 us  [on_device(): pl.pallas_call(kernel, out_shape=jax.ShapeDtypeStruct(velocity_tiles.shap...]
where the time goes in v3:
time: 116 us
  Pallas kernels  112 us (97%)
  other arithmetic  2.68 us (2%)
    pallas_call x1, Pallas kernels, on_device(): pl.pallas_call(kernel, out_shape=jax.ShapeDtypeStruct(velocity_tiles.shap...  112 us

profile of v3, /device:TPU:1, one launch (start us, length us, event | category | flops | bytes accessed | tf_op | source)
XLA Modules:
  0.0 115.6 jit_solution(4824897416009130617)
XLA Ops:
  0.0 0.0 copy-start
  0.7 0.0 copy-done
  0.8 0.2 dynamic-slice_reduce_fusion
  0.9 0.1 select_reduce_fusion
  1.0 0.7 broadcast_subtract_fusion.table
  1.7 112.0 %inversion.1 = f32[16,8,1024]{2,1,0:T(8,128)} custom-call(s32[4,32]{1,0:T(4,128)} %broadcast_subtract_fusion.table, s32[1]{0:T(128)S(6)} %copy.15.source_cell, f32[1,6]{1,0:T(1,128)} %wav.1, s32[1,256]{1,0:T(1,128)} %cells.1, f32[1,1536]{1,0:T(1,128)} %bitcast.1, f32[16,8,1024]{2,1,0:T(8,128)} %vel_at.1, f32[1,8,128,128]{3,2,1,0:T(8,128)} %early.1, ...), custom_call_target="tpu_custom_call" | custom-call | tf_op jit(solution)/shard_map/inversion/pallas_call | solution.py:631
  113.7 1.9 %broadcast_multiply_fusion = f32[16,8,1024]{2,1,0:T(8,128)} fusion(f32[16,8,1024]{2,1,0:T(8,128)} %inversion.1), kind=kLoop, calls=%fused_computation | loop fusion | flops 131072 | bytes 1048576 | tf_op jit(solution)/shard_map/mul | solution.py:692
  (5 shorter events, 0.0 us)
Async XLA Ops:
  0.0 0.7 copy-start

commit v4 on v3

--- a/solution.py
+++ b/solution.py
@@ -15,7 +15,7 @@
 BF16 = jnp.bfloat16
 PARTS = 2
 VEL_CUTS = (0, 6, 8)
-GRAD_CUTS = (0, 2, 8)
+GRAD_CUTS = (0, 3, 8)
 FACE_ORDER = (1, 2, 0, 3)
 Z_ORDER = (4, 3, 5, 2, 6, 1, 7, 0)
 

time: 116 us -> 117 us (level)
  no operation moved by 1% of the time
where the time goes in v4:
time: 117 us
  Pallas kernels  113 us (97%)
  other arithmetic  2.68 us (2%)
    pallas_call x1, Pallas kernels, on_device(): pl.pallas_call(kernel, out_shape=jax.ShapeDtypeStruct(velocity_tiles.shap...  113 us

profile of v4, /device:TPU:1, one launch (start us, length us, event | category | flops | bytes accessed | tf_op | source)
XLA Modules:
  0.0 116.6 jit_solution(7547711003777532047)
XLA Ops:
  0.0 0.0 copy-start
  0.7 0.0 copy-done
  0.8 0.2 dynamic-slice_reduce_fusion
  0.9 0.1 select_reduce_fusion
  1.0 0.7 broadcast_subtract_fusion.table
  1.7 113.0 %inversion.1 = f32[16,8,1024]{2,1,0:T(8,128)} custom-call(s32[4,32]{1,0:T(4,128)} %broadcast_subtract_fusion.table, s32[1]{0:T(128)S(6)} %copy.15.source_cell, f32[1,6]{1,0:T(1,128)} %wav.1, s32[1,256]{1,0:T(1,128)} %cells.1, f32[1,1536]{1,0:T(1,128)} %bitcast.1, f32[16,8,1024]{2,1,0:T(8,128)} %vel_at.1, f32[1,8,128,128]{3,2,1,0:T(8,128)} %early.1, ...), custom_call_target="tpu_custom_call" | custom-call | tf_op jit(solution)/shard_map/inversion/pallas_call | solution.py:631
  114.7 1.9 %broadcast_multiply_fusion = f32[16,8,1024]{2,1,0:T(8,128)} fusion(f32[16,8,1024]{2,1,0:T(8,128)} %inversion.1), kind=kLoop, calls=%fused_computation | loop fusion | flops 131072 | bytes 1048576 | tf_op jit(solution)/shard_map/mul | solution.py:692
  (5 shorter events, 0.0 us)
Async XLA Ops:
  0.0 0.7 copy-start
